TPU v7x, 256 devices: a whole 4x4x8 slice. The times are simulated.
256 devices in a mesh: seq: 128 (over y, z, x), head: 2 (over core).
Axes of the slice: x: 4, y: 4, z: 8, core: 2. Of those that a mesh axis runs over, the one named last changes fastest.
Arguments:
- queries: bfloat16 [8192, 1536], P('seq', 'head'), may hold values from -6 to 6
- key_vectors: bfloat16 [8192, 512], P('seq', 'head'), may hold values from -6 to 6
- value_vectors: bfloat16 [8192, 512], P('seq', 'head'), may hold values from -6 to 6
- lengths: int32 [64], replicated, may hold values from 1 to 256, 8192 in all
- out_weight: bfloat16 [1536, 1536], P('head', 'seq'), may hold values from -0.15625 to 0.15625
- residual: bfloat16 [8192, 1536], P(('seq', 'head')), may hold values from -6 to 6
- norm_gain: float32 [1536], replicated, may hold values from 0.1 to 1.9
- route_ids: int32 [8192, 6], P(('seq', 'head')), may hold values from 0 to 63, all different within a row; in each aligned block of 32 rows (0 to 31, 32 to 63, ...) at most 6 rows name the same one
- route_logits: float32 [8192, 6], P(('seq', 'head')), may hold values from -8 to 340
- shared_gate_up: bfloat16 [1536, 2, 1024], P(None, None, ('seq', 'head')), may hold values from -0.15625 to 0.15625
- shared_down: bfloat16 [1024, 1536], P(('seq', 'head')), may hold values from -0.1875 to 0.1875
- expert_gate_up: bfloat16 [128, 1536, 2, 256], P('seq'), may hold values from -0.15625 to 0.15625
- expert_down: bfloat16 [128, 256, 1536], P('seq'), may hold values from -0.25 to 0.25
- cache_blocks: bfloat16 [128, 128, 8, 4, 128], P('seq', None, None, 'head'), may hold values from -6 to 6
- block_table: int32 [128], replicated, may hold values from 0 to 127, each once
Outputs:
- layer_out: bfloat16 [8192, 1536], P(('seq', 'head'))
- cache_out: bfloat16 [128, 128, 8, 4, 128], P(None, 'seq', None, 'head')
Inputs may be any that keep to these rules, and one draw needn't show every extreme that they name: The lengths sum to 8192. `route_ids`: each token names 6 different experts; among the tokens of one device no expert is named more than 6 times. `block_table`: every block appears once.
All inputs are finite; a program needn't handle non-finite values.
Results may differ from a plain program's by a relative error of at most 0.0095.
Values may be sent and summed in bfloat16 or wider, within the bound.
A program may use at most 64 MiB of HBM per device.

v0:
```python
import math
import jax
import jax.numpy as jnp
from jax import lax
from jax.sharding import PartitionSpec as P

HD = 128
EXPERTS = 64
TOP = 6
REACH = 4
HALVES = 128
CAP = 6
NEGATIVE = -1e30
EPSILON = 1e-05


def from_behind(shard, axis, by):
    devices = lax.axis_size(axis)
    pairs = [(i, i + by) for i in range(devices) if 0 <= i + by < devices]
    return lax.ppermute(shard, axis, pairs)


def segment_of(positions, lengths):
    request_ends = jnp.cumsum(lengths)
    passed = (request_ends[None, :] <= positions[:, None]).astype(jnp.int32)
    return jnp.sum(passed, axis=1)


def shared_ffn(rows_in, gate_up_part, down_part):
    shared_both = jnp.einsum(
        "td,dcf->tcf", rows_in, gate_up_part, preferred_element_type=jnp.float32
    )
    shared_act = (jax.nn.silu(shared_both[:, 0]) * shared_both[:, 1]).astype(jnp.bfloat16)
    return jnp.dot(shared_act, down_part, preferred_element_type=jnp.float32)


def shards(
    queries,
    key_vectors,
    value_vectors,
    lengths,
    out_weight,
    residual,
    norm_gain,
    route_ids,
    route_logits,
    shared_gate_up,
    shared_down,
    expert_gate_up,
    expert_down,
    cache_blocks,
    block_table,
):
    handed = lax.all_to_all(cache_blocks, "seq", split_axis=1, concat_axis=0, tiled=True)
    cache_out = jnp.take(handed, block_table, axis=0)
    tok_rows = queries.shape[0]
    seq_index = lax.axis_index("seq")
    earlier = [
        from_behind((key_vectors, value_vectors), "seq", offset) for offset in range(REACH, 0, -1)
    ]
    window_keys = jnp.concatenate([member[0] for member in earlier] + [key_vectors], axis=0)
    window_values = jnp.concatenate([member[1] for member in earlier] + [value_vectors], axis=0)
    key_count = window_keys.shape[0]
    kv_heads = key_vectors.shape[1] // HD
    query_heads = queries.shape[1] // HD
    group_size = query_heads // kv_heads
    query_pos = seq_index * tok_rows + jnp.arange(tok_rows, dtype=jnp.int32)
    key_pos = (seq_index - REACH) * tok_rows + jnp.arange(key_count, dtype=jnp.int32)
    visible = (key_pos[None, :] >= 0) & (key_pos[None, :] <= query_pos[:, None])
    visible = visible & (
        segment_of(key_pos, lengths)[None, :] == segment_of(query_pos, lengths)[:, None]
    )
    query_part = queries.reshape(tok_rows, kv_heads, group_size, HD)
    key_part = window_keys.reshape(key_count, kv_heads, HD)
    value_part = window_values.reshape(key_count, kv_heads, HD)
    scores = jnp.einsum(
        "tkgd,wkd->kgtw", query_part, key_part, preferred_element_type=jnp.float32
    ) * (1.0 / math.sqrt(HD))
    scores = jnp.where(visible[None, None], scores, NEGATIVE)
    row_max = jnp.max(scores, axis=-1, keepdims=True)
    weights = jnp.exp(scores - row_max)
    row_total = jnp.sum(weights, axis=-1)
    weighted = jnp.einsum(
        "kgtw,wkd->tkgd",
        weights.astype(jnp.bfloat16),
        value_part,
        preferred_element_type=jnp.float32,
    )
    heads = (weighted / jnp.transpose(row_total, (2, 0, 1))[..., None]).astype(jnp.bfloat16)
    heads = heads.reshape(tok_rows, query_heads * HD)
    partial_out = jnp.dot(
        heads,
        lax.all_gather(out_weight, "seq", axis=1, tiled=True),
        preferred_element_type=jnp.float32,
    )
    attn_out = lax.psum_scatter(partial_out, "head", scatter_dimension=0, tiled=True)
    mixed = residual.astype(jnp.float32) + attn_out
    mean_square = jnp.mean(mixed * mixed, axis=-1, keepdims=True)
    normed = (mixed * lax.rsqrt(mean_square + EPSILON) * norm_gain).astype(jnp.bfloat16)
    gate_up_all, down_all = (
        lax.all_gather(shared_gate_up, ("seq", "head"), axis=2, tiled=True),
        lax.all_gather(shared_down, ("seq", "head"), axis=0, tiled=True),
    )
    shared_part = shared_ffn(normed, gate_up_all, down_all)
    own_tokens = normed.shape[0]
    width_model = normed.shape[1]
    flat_ids = route_ids.reshape(-1)
    onehot = (flat_ids[:, None] == jnp.arange(EXPERTS, dtype=jnp.int32)[None, :]).astype(jnp.int32)
    slot_rank = jnp.sum((jnp.cumsum(onehot, axis=0) - 1) * onehot, axis=1)
    first_slot = flat_ids * CAP + slot_rank
    second_slot = (flat_ids + EXPERTS) * CAP + slot_rank
    token_of = jnp.arange(flat_ids.shape[0], dtype=jnp.int32) // TOP
    routed_rows = normed[token_of]
    outgoing = jnp.zeros((HALVES * CAP, width_model), jnp.bfloat16)
    outgoing = outgoing.at[jnp.concatenate([first_slot, second_slot])].set(
        jnp.concatenate([routed_rows, routed_rows], axis=0)
    )
    local_halves = expert_gate_up.shape[0]
    outgoing = outgoing.reshape(HALVES // local_halves, local_halves, CAP, width_model)
    gate_up = jnp.einsum(
        "nsjd,sdcf->nsjcf",
        lax.all_to_all(outgoing, "seq", split_axis=0, concat_axis=0, tiled=True),
        expert_gate_up,
        preferred_element_type=jnp.float32,
    )
    expert_act = (jax.nn.silu(gate_up[:, :, :, 0]) * gate_up[:, :, :, 1]).astype(jnp.bfloat16)
    half_out = jnp.einsum(
        "nsjf,sfd->nsjd", expert_act, expert_down, preferred_element_type=jnp.float32
    ).astype(jnp.bfloat16)
    returned = lax.all_to_all(half_out, "seq", split_axis=0, concat_axis=0, tiled=True)
    returned = returned.reshape(HALVES * CAP, width_model)
    pair_sum = returned[first_slot].astype(jnp.float32) + returned[second_slot].astype(jnp.float32)
    route_probs = jax.nn.softmax(route_logits, axis=-1)
    routed = jnp.sum(
        route_probs[:, :, None] * pair_sum.reshape(own_tokens, TOP, width_model), axis=1
    )
    layer_out = (mixed + shared_part + routed).astype(jnp.bfloat16)
    return (layer_out, cache_out)


def solution(mesh):
    in_specs = (
        P("seq", "head"),
        P("seq", "head"),
        P("seq", "head"),
        P(),
        P("head", "seq"),
        P(("seq", "head"), None),
        P(),
        P(("seq", "head"), None),
        P(("seq", "head"), None),
        P(None, None, ("seq", "head")),
        P(("seq", "head"), None),
        P("seq", None, None, None),
        P("seq", None, None),
        P("seq", None, None, "head", None),
        P(),
    )
    out_specs = (P(("seq", "head"), None), P(None, "seq", None, "head", None))
    return jax.shard_map(shards, mesh=mesh, in_specs=in_specs, out_specs=out_specs, check_vma=False)
```

profile of v0, /device:TPU:1, one launch (start us, length us, event | category | flops | bytes accessed | tf_op | source)
XLA Modules:
  0.0 410.7 jit_solution(4338545764262982124)
XLA Ops:
  8.1 0.7 all-gather.8.cloned.1.call-update
  8.8 4.4 %collective-permute-start.4 = (bf16[64,256]{1,0:T(8,128)(2,1)}, bf16[64,256]{1,0:T(8,128)(2,1)S(1)}, u32[]{:S(2)}, u32[]{:S(2)}) collective-permute-start(bf16[64,256]{1,0:T(8,128)(2,1)} %param.16), channel_id=1, source_target_pairs={{0,8},{2,10},{4,12},{6,14},{8,16},{10,18},{12,20},{14,22},{16,24},... | collective-permute-start | bytes 98312 | tf_op jit(solution)/shard_map/ppermute | solution.py:20
  13.2 4.4 %collective-permute-start.5 = (bf16[64,256]{1,0:T(8,128)(2,1)}, bf16[64,256]{1,0:T(8,128)(2,1)S(1)}, u32[]{:S(2)}, u32[]{:S(2)}) collective-permute-start(bf16[64,256]{1,0:T(8,128)(2,1)} %param.16), channel_id=1, source_target_pairs={{0,6},{2,8},{4,10},{6,12},{8,14},{10,16},{12,18},{14,20},{16,22},{... | collective-permute-start | bytes 98312 | tf_op jit(solution)/shard_map/ppermute | solution.py:20
  17.6 3.8 collective-permute-start.6
  21.4 2.5 collective-permute-start.7
  23.9 3.6 collective-permute-start
  27.4 0.7 copy.54
  28.2 0.1 reduce-window.18
  28.3 0.1 reduce
  28.4 0.2 convert_reduce_fusion.1
  28.6 0.1 convert_reduce_fusion
  28.7 0.1 compare_and_fusion
  28.8 0.9 reshape.398
  29.8 6.5 %collective-permute-start.1 = (bf16[64,256]{1,0:T(8,128)(2,1)}, bf16[64,256]{1,0:T(8,128)(2,1)S(1)}, u32[]{:S(2)}, u32[]{:S(2)}) collective-permute-start(bf16[64,256]{1,0:T(8,128)(2,1)} %param.17), channel_id=1, source_target_pairs={{0,6},{2,8},{4,10},{6,12},{8,14},{10,16},{12,18},{14,20},{16,22},{... | collective-permute-start | bytes 98312 | tf_op jit(solution)/shard_map/ppermute | solution.py:20
  36.4 3.1 collective-permute-start.2
  39.5 1.4 collective-permute-start.3
  40.9 0.8 constant_dynamic-update-slice_fusion.5
  41.8 0.4 collective-permute-done.3
  42.2 0.8 constant_dynamic-update-slice_fusion
  43.0 0.3 fusion.48
  43.4 0.2 fusion.27
  43.6 0.3 fusion.23
  43.9 0.1 copy.58
  44.1 83.4 %all-gather.8.cloned.1.call-done = bf16[128,12,768]{2,1,0:T(8,128)(2,1)} async-done(((bf16[1,12,768]{2,1,0:T(8,128)(2,1)}), bf16[128,12,768]{2,1,0:T(8,128)(2,1)}) %all-gather.8.cloned.1.call-update) | async-done | bytes 2359312 | tf_op jit(solution)/shard_map/all_gather | solution.py:93
  127.5 3.6 reshape.454
  131.2 1.6 fusion.49
  132.8 0.5 all-gather.10.cloned.1.call-update
  133.4 0.6 copy.59
  134.1 0.1 copy.62
  134.2 0.1 reshape.400
  134.3 0.6 reduce-window.19
  134.9 0.2 slice_reduce_fusion
  135.2 0.1 bitcast_bitcast_fusion
  135.3 0.1 fusion.45
  135.4 12.7 %reduce-scatter.2.cloned.1.call-done = f32[32,1536]{1,0:T(8,128)} async-done(((f32[64,1536]{1,0:T(8,128)}), f32[32,1536]{1,0:T(8,128)}) %reduce-scatter.2.cloned.1.call-update) | async-done | bytes 196624 | tf_op jit(solution)/shard_map/reduce_scatter | solution.py:96
  148.1 1.1 multiply_reduce_fusion.1
  149.2 1.0 multiply_convert_fusion
  150.2 1.9 gather_fusion
  152.1 3.9 scatter_custom_fusion
  156.0 2.5 reshape.403
  158.5 89.1 %all_to_all.22 = bf16[128,1,6,1536]{3,2,1,0:T(8,128)(2,1)} all-to-all(bf16[128,1,6,1536]{3,2,1,0:T(8,128)(2,1)} %bitcast.96), channel_id=1, replica_groups=mesh['seq'=128,'head'=2] {'seq'}, dimensions={0} | all-to-all | bytes 4718592 | tf_op jit(solution)/shard_map/all_to_all | solution.py:122
  247.6 10.7 %all-to-all-start.2 = ((bf16[1,128,8,2,128]{4,3,2,0,1:T(2,128)(2,1)}), bf16[1,128,8,2,128]{4,3,2,0,1:T(2,128)(2,1)S(1)}, u32[]{:S(2)}, u32[]{:S(2)}) async-start(bf16[1,128,8,2,128]{4,3,2,0,1:T(2,128)(2,1)} %bitcast.36), calls=%async_computation.3 | async-start | bytes 1048576 | tf_op jit(solution)/shard_map/all_to_all | solution.py:54
  258.3 3.3 fusion.10
  261.6 0.8 fusion.2
  262.4 3.0 copy.68
  265.3 9.3 %all-to-all-done.2 = bf16[1,128,8,2,128]{4,3,2,0,1:T(2,128)(2,1)S(1)} async-done(((bf16[1,128,8,2,128]{4,3,2,0,1:T(2,128)(2,1)}), bf16[1,128,8,2,128]{4,3,2,0,1:T(2,128)(2,1)S(1)}, u32[]{:S(2)}, u32[]{:S(2)}) %all-to-all-start.2) | async-done | bytes 524320 | tf_op jit(solution)/shard_map/all_to_all | solution.py:54
  274.6 8.9 %all-to-all-start.1 = ((bf16[128,1,6,1536]{3,2,1,0:T(8,128)(2,1)}), bf16[128,1,6,1536]{3,2,1,0:T(8,128)(2,1)}, u32[]{:S(2)}, u32[]{:S(2)}) async-start(bf16[128,1,6,1536]{3,2,1,0:T(8,128)(2,1)} %copy.68), calls=%async_computation.2 | async-start | bytes 6291456 | tf_op jit(solution)/shard_map/all_to_all | solution.py:130
  283.6 0.1 copy.69
  283.7 0.1 mul.140
  283.8 0.1 copy.70
  283.9 0.1 mul.142
  284.0 0.1 copy.61
  284.2 1.6 gather_fusion.3
  285.8 1.4 fusion.26
  287.2 5.9 %reshape.456 = bf16[1024,1536]{1,0:T(8,128)(2,1)} reshape(bf16[256,4,1536]{2,1,0:T(4,128)(2,1)} %all-gather.10.cloned.1.call-done) | data formatting | bytes 6291456
  293.1 91.6 %all-gather.6.cloned.1.call-done = bf16[1536,2,1024]{0,1,2:T(2,128)(2,1)} async-done(((bf16[1536,2,4]{0,1,2:T(2,128)(2,1)}), bf16[1536,2,1024]{0,1,2:T(2,128)(2,1)}) %all-gather.6.cloned.1.call-update) | async-done | bytes 6291472 | tf_op jit(solution)/shard_map/all_gather | solution.py:101
  384.8 5.5 %fusion = f32[32,2,1024]{2,0,1:T(8,128)} fusion(bf16[1536,2,1024]{0,1,2:T(2,128)(2,1)} %all-gather.6.cloned.1.call-done, bf16[32,1536]{1,0:T(8,128)(2,1)S(1)} %multiply_convert_fusion), kind=kOutput, calls=%fused_computation.5 | convolution fusion | flops 201326592 | bytes 6651904 | tf_op jit(solution)/shard_map/td,dcf->tcf/dot_general | solution.py:30
  390.2 3.7 reshape.407
  393.9 1.9 gather_fusion.1
  395.8 1.9 gather_fusion.2
  397.7 1.4 convert_add_fusion
  399.1 0.2 add.235
  399.3 0.6 multiply_reduce_fusion
  399.8 3.4 fusion.7
  (63 shorter events, 0.7 us)
Async XLA Ops:
  8.0 253.6 %copy-start = (bf16[1,256,1536]{2,1,0:T(8,128)(2,1)S(1)}, bf16[1,256,1536]{2,1,0:T(8,128)(2,1)}, u32[]{:S(2)}) copy-start(bf16[1,256,1536]{2,1,0:T(8,128)(2,1)} %param.27) | copy-start | bytes 2359300
  8.0 119.5 %all-gather.8.cloned.1.call-start = ((), (), s32[]{:S(2)}) async-start(), calls=%async_computation.6 | async-start | bytes 3170304 | tf_op jit(solution)/shard_map/all_gather | solution.py:93
  8.7 139.4 %reduce-scatter.2.cloned.1.call-start = ((), (), s32[]{:S(2)}) async-start(), calls=%async_computation.4 | async-start | bytes 589824 | tf_op jit(solution)/shard_map/reduce_scatter | solution.py:96
  8.8 21.0 %collective-permute-start.4 = (bf16[64,256]{1,0:T(8,128)(2,1)}, bf16[64,256]{1,0:T(8,128)(2,1)S(1)}, u32[]{:S(2)}, u32[]{:S(2)}) collective-permute-start(bf16[64,256]{1,0:T(8,128)(2,1)} %param.16), channel_id=1, source_target_pairs={{0,8},{2,10},{4,12},{6,14},{8,16},{10,18},{12,20},{14,22},{16,24},... | collective-permute-start | bytes 98312 | tf_op jit(solution)/shard_map/ppermute | solution.py:20
  13.2 23.2 %collective-permute-start.5 = (bf16[64,256]{1,0:T(8,128)(2,1)}, bf16[64,256]{1,0:T(8,128)(2,1)S(1)}, u32[]{:S(2)}, u32[]{:S(2)}) collective-permute-start(bf16[64,256]{1,0:T(8,128)(2,1)} %param.16), channel_id=1, source_target_pairs={{0,6},{2,8},{4,10},{6,12},{8,14},{10,16},{12,18},{14,20},{16,22},{... | collective-permute-start | bytes 98312 | tf_op jit(solution)/shard_map/ppermute | solution.py:20
  17.6 22.0 %collective-permute-start.6 = (bf16[64,256]{1,0:T(8,128)(2,1)}, bf16[64,256]{1,0:T(8,128)(2,1)S(1)}, u32[]{:S(2)}, u32[]{:S(2)}) collective-permute-start(bf16[64,256]{1,0:T(8,128)(2,1)} %param.16), channel_id=1, source_target_pairs={{0,4},{2,6},{4,8},{6,10},{8,12},{10,14},{12,16},{14,18},{16,20},{1... | collective-permute-start | bytes 98312 | tf_op jit(solution)/shard_map/ppermute | solution.py:20
  21.4 19.5 %collective-permute-start.7 = (bf16[64,256]{1,0:T(8,128)(2,1)}, bf16[64,256]{1,0:T(8,128)(2,1)S(1)}, u32[]{:S(2)}, u32[]{:S(2)}) collective-permute-start(bf16[64,256]{1,0:T(8,128)(2,1)} %param.16), channel_id=1, source_target_pairs={{0,2},{2,4},{4,6},{6,8},{8,10},{10,12},{12,14},{14,16},{16,18},{18... | collective-permute-start | bytes 98312 | tf_op jit(solution)/shard_map/ppermute | solution.py:20
  23.9 17.8 %collective-permute-start = (bf16[64,256]{1,0:T(8,128)(2,1)}, bf16[64,256]{1,0:T(8,128)(2,1)S(1)}, u32[]{:S(2)}, u32[]{:S(2)}) collective-permute-start(bf16[64,256]{1,0:T(8,128)(2,1)} %param.17), channel_id=1, source_target_pairs={{0,8},{2,10},{4,12},{6,14},{8,16},{10,18},{12,20},{14,22},{16,24},... | collective-permute-start | bytes 98312 | tf_op jit(solution)/shard_map/ppermute | solution.py:20
  29.8 11.9 %collective-permute-start.1 = (bf16[64,256]{1,0:T(8,128)(2,1)}, bf16[64,256]{1,0:T(8,128)(2,1)S(1)}, u32[]{:S(2)}, u32[]{:S(2)}) collective-permute-start(bf16[64,256]{1,0:T(8,128)(2,1)} %param.17), channel_id=1, source_target_pairs={{0,6},{2,8},{4,10},{6,12},{8,14},{10,16},{12,18},{14,20},{16,22},{... | collective-permute-start | bytes 98312 | tf_op jit(solution)/shard_map/ppermute | solution.py:20
  36.4 5.4 %collective-permute-start.2 = (bf16[64,256]{1,0:T(8,128)(2,1)}, bf16[64,256]{1,0:T(8,128)(2,1)S(1)}, u32[]{:S(2)}, u32[]{:S(2)}) collective-permute-start(bf16[64,256]{1,0:T(8,128)(2,1)} %param.17), channel_id=1, source_target_pairs={{0,4},{2,6},{4,8},{6,10},{8,12},{10,14},{12,16},{14,18},{16,20},{1... | collective-permute-start | bytes 98312 | tf_op jit(solution)/shard_map/ppermute | solution.py:20
  39.5 2.7 collective-permute-start.3
  131.1 2.3 copy-start.3
  131.1 2.9 copy-start.4
  131.2 16.9 %copy-start.1 = (bf16[32,1536]{1,0:T(8,128)(2,1)S(1)}, bf16[32,1536]{1,0:T(8,128)(2,1)}, u32[]{:S(2)}) copy-start(bf16[32,1536]{1,0:T(8,128)(2,1)} %param.20) | copy-start | bytes 294916
  131.2 18.0 %copy-start.5 = (f32[1536]{0:T(1024)S(1)}, f32[1536]{0:T(1024)}, u32[]{:S(2)}) copy-start(f32[1536]{0:T(1024)} %param.21) | copy-start | bytes 18436
  132.8 154.4 %all-gather.10.cloned.1.call-start = ((), (), s32[]{:S(2)}) async-start(), calls=%async_computation.7 | async-start | bytes 3158016 | tf_op jit(solution)/shard_map/all_gather | solution.py:102
  133.4 251.4 %all-gather.6.cloned.1.call-start = ((), (), s32[]{:S(2)}) async-start(), calls=%async_computation.5 | async-start | bytes 6316032 | tf_op jit(solution)/shard_map/all_gather | solution.py:101
  158.5 99.8 %copy-start.6 = (bf16[1,1536,2,256]{3,2,1,0:T(2,128)(2,1)S(1)}, bf16[1,1536,2,256]{3,2,1,0:T(2,128)(2,1)}, u32[]{:S(2)}) copy-start(bf16[1,1536,2,256]{3,2,1,0:T(2,128)(2,1)} %param.26) | copy-start | bytes 4718596
  247.6 27.1 %all-to-all-start.2 = ((bf16[1,128,8,2,128]{4,3,2,0,1:T(2,128)(2,1)}), bf16[1,128,8,2,128]{4,3,2,0,1:T(2,128)(2,1)S(1)}, u32[]{:S(2)}, u32[]{:S(2)}) async-start(bf16[1,128,8,2,128]{4,3,2,0,1:T(2,128)(2,1)} %bitcast.36), calls=%async_computation.3 | async-start | bytes 1048576 | tf_op jit(solution)/shard_map/all_to_all | solution.py:54
  265.3 18.6 %copy-start.2 = (f32[32,6]{0,1:T(8,128)S(1)}, f32[32,6]{0,1:T(8,128)}, u32[]{:S(2)}) copy-start(f32[32,6]{0,1:T(8,128)} %param.23) | copy-start | bytes 2308
  265.3 18.8 %copy-start.7 = (s32[128]{0:T(128)S(1)}, s32[128]{0:T(128)}, u32[]{:S(2)}) copy-start(s32[128]{0:T(128)} %param.29) | copy-start | bytes 1540
  274.6 115.6 %all-to-all-start.1 = ((bf16[128,1,6,1536]{3,2,1,0:T(8,128)(2,1)}), bf16[128,1,6,1536]{3,2,1,0:T(8,128)(2,1)}, u32[]{:S(2)}, u32[]{:S(2)}) async-start(bf16[128,1,6,1536]{3,2,1,0:T(8,128)(2,1)} %copy.68), calls=%async_computation.2 | async-start | bytes 6291456 | tf_op jit(solution)/shard_map/all_to_all | solution.py:130
Sparse Core Ops, SparseCore 0:
  12.5 114.9 all-gather.7
  132.9 15.1 reduce-scatter.1
Sparse Core Ops, SparseCore 1:
  137.6 121.0 all-gather.9
  263.6 121.1 all-gather.5
where the time goes:
time: 412 us; the launch traced here: 411 us
  waiting for transfers between devices  199 us (48%)
  blocking collectives  89.1 us (22%)
  starting transfers between devices  49.4 us (12%)
  local copies, waits for them, and re-layouts  31.2 us (8%)
  between operations  16 us (4%)
  matrix products  15.2 us (4%)
  other arithmetic  11.1 us (3%)
    all_gather x1, waiting for transfers between devices, shards(): lax.all_gather(shared_gate_up, ('seq', 'head'), axis=2, tiled=True)  91.6 us
    all_to_all x1, blocking collectives, shards(): lax.all_to_all(outgoing, 'seq', split_axis=0, concat_axis=0, tiled=True)  89.1 us
    all_gather x1, waiting for transfers between devices, shards(): lax.all_gather(out_weight, 'seq', axis=1, tiled=True)  83.4 us
    ppermute x8, starting transfers between devices, from_behind(): return lax.ppermute(shard, axis, pairs)  29.7 us
    reduce_scatter x1, waiting for transfers between devices, shards(): lax.psum_scatter(partial_out, 'head', scatter_dimension=0, tiled=True)  12.7 us
    all_to_all x1, starting transfers between devices, shards(): lax.all_to_all(cache_blocks, 'seq', split_axis=1, concat_axis=0, tiled=True)  10.7 us
    unnamed x28, local copies, waits for them, and re-layouts  10.3 us
    all_to_all x1, waiting for transfers between devices, shards(): lax.all_to_all(cache_blocks, 'seq', split_axis=1, concat_axis=0, tiled=True)  9.29 us
  transfers between devices with their start and end apart: 14, of which 5 were waited for; matrix products, arithmetic and copies ran while one was open for 10% of the time, Pallas kernels for 0%

commit v1 on v0

--- a/solution.py
+++ b/solution.py
@@ -51,7 +51,9 @@
     cache_blocks,
     block_table,
 ):
-    handed = lax.all_to_all(cache_blocks, "seq", split_axis=1, concat_axis=0, tiled=True)
+    pieces = jnp.split(cache_blocks, lax.axis_size("seq"), axis=1)
+    received = lax.all_to_all(jnp.stack(pieces), "seq", 0, 0)
+    handed = jnp.concatenate(received, axis=0)
     cache_out = jnp.take(handed, block_table, axis=0)
     tok_rows = queries.shape[0]
     seq_index = lax.axis_index("seq")

time: 412 us -> 504 us (1.22)
  the two profiles are of different devices: /device:TPU:1 before, /device:TPU:32 now
where the time goes in v1:
time: 504 us; the launch traced here: 499 us
  waiting for transfers between devices  204 us (40%)
  local copies, waits for them, and re-layouts  195 us (39%)
  starting transfers between devices  56.9 us (11%)
  between operations  16.1 us (3%)
  matrix products  15.2 us (3%)
  other arithmetic  11.1 us (2%)
    unnamed x155, local copies, waits for them, and re-layouts  173 us
    all_gather x1, waiting for transfers between devices, shards(): lax.all_gather(out_weight, 'seq', axis=1, tiled=True)  79.6 us
    all_to_all x1, waiting for transfers between devices, shards(): lax.all_to_all(outgoing, 'seq', split_axis=0, concat_axis=0, tiled=True)  56.2 us
    all_to_all x1, waiting for transfers between devices, shards(): lax.all_to_all(half_out, 'seq', split_axis=0, concat_axis=0, tiled=True)  54 us
    ppermute x8, starting transfers between devices, from_behind(): return lax.ppermute(shard, axis, pairs)  30.5 us
    all_to_all x1, starting transfers between devices, shards(): lax.all_to_all(outgoing, 'seq', split_axis=0, concat_axis=0, tiled=True)  11.2 us
  transfers between devices with their start and end apart: 15, of which 6 were waited for; matrix products, arithmetic and copies ran while one was open for 41% of the time, Pallas kernels for 0%

profile of v1, /device:TPU:32, one launch (start us, length us, event | category | flops | bytes accessed | tf_op | source)
XLA Modules:
  0.0 498.8 jit_solution(3453965950669839138)
XLA Ops:
  8.8 3.8 collective-permute-start.4
  12.6 4.7 collective-permute-start.5
  17.3 4.1 collective-permute-start.6
  21.4 2.8 collective-permute-start.7
  24.2 5.0 %collective-permute-start = (bf16[64,256]{1,0:T(8,128)(2,1)}, bf16[64,256]{1,0:T(8,128)(2,1)S(1)}, u32[]{:S(2)}, u32[]{:S(2)}) collective-permute-start(bf16[64,256]{1,0:T(8,128)(2,1)} %param.17), channel_id=1, source_target_pairs={{0,8},{2,10},{4,12},{6,14},{8,16},{10,18},{12,20},{14,22},{16,24},... | collective-permute-start | bytes 98312 | tf_op jit(solution)/shard_map/ppermute | solution.py:20
  31.6 4.7 collective-permute-start.1
  36.3 3.4 collective-permute-start.2
  39.8 1.9 collective-permute-start.3
  42.5 2.5 collective-permute-done.2
  45.1 2.8 collective-permute-done.3
  49.8 79.6 %all-gather.8.cloned.1.call-done = bf16[128,12,768]{2,1,0:T(8,128)(2,1)} async-done(((bf16[1,12,768]{2,1,0:T(8,128)(2,1)}), bf16[128,12,768]{2,1,0:T(8,128)(2,1)}) %all-gather.8.cloned.1.call-update) | async-done | bytes 2359312 | tf_op jit(solution)/shard_map/all_gather | solution.py:95
  129.4 3.6 reshape.455
  133.0 1.6 fusion.48
  137.2 1.3 constant_dynamic-update-slice_fusion.137
  138.4 1.3 constant_dynamic-update-slice_fusion.136
  139.7 1.3 constant_dynamic-update-slice_fusion.135
  142.3 1.3 constant_dynamic-update-slice_fusion.133
  143.6 1.3 constant_dynamic-update-slice_fusion.132
  144.9 1.3 constant_dynamic-update-slice_fusion.131
  146.1 1.3 constant_dynamic-update-slice_fusion.130
  147.4 1.3 constant_dynamic-update-slice_fusion.129
  148.7 1.3 constant_dynamic-update-slice_fusion.128
  150.0 1.3 constant_dynamic-update-slice_fusion.127
  151.3 1.3 constant_dynamic-update-slice_fusion.126
  153.8 1.3 constant_dynamic-update-slice_fusion.124
  155.1 1.3 constant_dynamic-update-slice_fusion.123
  157.7 1.3 constant_dynamic-update-slice_fusion.121
  159.0 1.3 constant_dynamic-update-slice_fusion.120
  160.3 1.3 constant_dynamic-update-slice_fusion.119
  161.6 1.3 constant_dynamic-update-slice_fusion.118
  162.8 1.3 constant_dynamic-update-slice_fusion.117
  164.1 1.3 constant_dynamic-update-slice_fusion.116
  165.4 1.3 constant_dynamic-update-slice_fusion.115
  168.0 1.3 constant_dynamic-update-slice_fusion.113
  169.3 1.3 constant_dynamic-update-slice_fusion.112
  170.5 1.3 constant_dynamic-update-slice_fusion.111
  191.1 1.3 constant_dynamic-update-slice_fusion.95
  205.2 1.3 constant_dynamic-update-slice_fusion.84
  221.9 1.3 constant_dynamic-update-slice_fusion.71
  259.1 1.3 constant_dynamic-update-slice_fusion.42
  265.6 1.3 constant_dynamic-update-slice_fusion.37
  276.7 1.9 gather_fusion
  278.6 3.9 scatter_custom_fusion
  282.5 2.5 reshape.403
  285.0 11.2 %all-to-all-start = ((bf16[128,1,6,1536]{3,2,1,0:T(8,128)(2,1)}), bf16[128,1,6,1536]{3,2,1,0:T(8,128)(2,1)}, u32[]{:S(2)}, u32[]{:S(2)}) async-start(bf16[128,1,6,1536]{3,2,1,0:T(8,128)(2,1)} %bitcast.347), calls=%async_computation.1 | async-start | bytes 6291456 | tf_op jit(solution)/shard_map/all_to_all | solution.py:124
  296.3 1.3 constant_dynamic-update-slice_fusion.30
  301.4 1.3 constant_dynamic-update-slice_fusion.26
  321.9 1.3 constant_dynamic-update-slice_fusion.10
  323.2 56.2 %all-to-all-done = bf16[128,1,6,1536]{3,2,1,0:T(8,128)(2,1)} async-done(((bf16[128,1,6,1536]{3,2,1,0:T(8,128)(2,1)}), bf16[128,1,6,1536]{3,2,1,0:T(8,128)(2,1)}, u32[]{:S(2)}, u32[]{:S(2)}) %all-to-all-start) | async-done | bytes 2359328 | tf_op jit(solution)/shard_map/all_to_all | solution.py:124
  379.4 7.3 %all-to-all-start.2 = ((bf16[128,1,1,8,2,128]{5,4,3,2,1,0:T(2,128)(2,1)}), bf16[128,1,1,8,2,128]{5,4,3,2,1,0:T(2,128)(2,1)S(1)}, u32[]{:S(2)}, u32[]{:S(2)}) async-start(bf16[128,1,1,8,2,128]{5,4,3,2,1,0:T(2,128)(2,1)} %constant_dynamic-update-slice_fusion.10), calls=%async_computation.3 | async-start | bytes 1048576 | tf_op jit(solution)/shard_map/all_to_all | solution.py:55
  386.7 3.3 fusion.10
  390.8 3.0 copy.66
  393.8 7.8 %all-to-all-done.2 = bf16[128,1,1,8,2,128]{5,4,3,2,1,0:T(2,128)(2,1)S(1)} async-done(((bf16[128,1,1,8,2,128]{5,4,3,2,1,0:T(2,128)(2,1)}), bf16[128,1,1,8,2,128]{5,4,3,2,1,0:T(2,128)(2,1)S(1)}, u32[]{:S(2)}, u32[]{:S(2)}) %all-to-all-start.2) | async-done | bytes 524320 | tf_op jit(solution)/shard_map/all_to_all | solution.py:55
  401.6 7.8 %all-to-all-start.1 = ((bf16[128,1,6,1536]{3,2,1,0:T(8,128)(2,1)}), bf16[128,1,6,1536]{3,2,1,0:T(8,128)(2,1)}, u32[]{:S(2)}, u32[]{:S(2)}) async-start(bf16[128,1,6,1536]{3,2,1,0:T(8,128)(2,1)} %copy.66), calls=%async_computation.2 | async-start | bytes 6291456 | tf_op jit(solution)/shard_map/all_to_all | solution.py:132
  410.0 1.6 gather_fusion.3
  411.7 1.4 broadcast_select_fusion
  413.0 5.9 %reshape.457 = bf16[1024,1536]{1,0:T(8,128)(2,1)} reshape(bf16[256,4,1536]{2,1,0:T(4,128)(2,1)} %all-gather.10.cloned.1.call-done) | data formatting | bytes 6291456
  418.9 5.5 %fusion = f32[32,2,1024]{2,0,1:T(8,128)} fusion(bf16[1536,2,1024]{0,1,2:T(2,128)(2,1)} %all-gather.6.cloned.1.call-done, bf16[32,1536]{1,0:T(8,128)(2,1)S(1)} %multiply_convert_fusion), kind=kOutput, calls=%fused_computation.5 | convolution fusion | flops 201326592 | bytes 6651904 | tf_op jit(solution)/shard_map/td,dcf->tcf/dot_general | solution.py:30
  424.4 54.0 %all-to-all-done.1 = bf16[128,1,6,1536]{3,2,1,0:T(8,128)(2,1)} async-done(((bf16[128,1,6,1536]{3,2,1,0:T(8,128)(2,1)}), bf16[128,1,6,1536]{3,2,1,0:T(8,128)(2,1)}, u32[]{:S(2)}, u32[]{:S(2)}) %all-to-all-start.1) | async-done | bytes 2359328 | tf_op jit(solution)/shard_map/all_to_all | solution.py:132
  478.4 3.7 reshape.407
  482.1 1.9 gather_fusion.1
  483.9 1.9 gather_fusion.2
  485.8 1.4 convert_add_fusion
  488.0 3.4 fusion.7
  (192 shorter events, 137.0 us)
Async XLA Ops:
  8.0 382.0 %copy-start = (bf16[1,256,1536]{2,1,0:T(8,128)(2,1)S(1)}, bf16[1,256,1536]{2,1,0:T(8,128)(2,1)}, u32[]{:S(2)}) copy-start(bf16[1,256,1536]{2,1,0:T(8,128)(2,1)} %param.27) | copy-start | bytes 2359300
  8.0 121.3 %all-gather.8.cloned.1.call-start = ((), (), s32[]{:S(2)}) async-start(), calls=%async_computation.6 | async-start | bytes 3170304 | tf_op jit(solution)/shard_map/all_gather | solution.py:95
  8.7 265.9 %reduce-scatter.2.cloned.1.call-start = ((), (), s32[]{:S(2)}) async-start(), calls=%async_computation.4 | async-start | bytes 589824 | tf_op jit(solution)/shard_map/reduce_scatter | solution.py:98
  8.8 22.8 %collective-permute-start.4 = (bf16[64,256]{1,0:T(8,128)(2,1)}, bf16[64,256]{1,0:T(8,128)(2,1)S(1)}, u32[]{:S(2)}, u32[]{:S(2)}) collective-permute-start(bf16[64,256]{1,0:T(8,128)(2,1)} %param.16), channel_id=1, source_target_pairs={{0,8},{2,10},{4,12},{6,14},{8,16},{10,18},{12,20},{14,22},{16,24},... | collective-permute-start | bytes 98312 | tf_op jit(solution)/shard_map/ppermute | solution.py:20
  12.6 23.7 %collective-permute-start.5 = (bf16[64,256]{1,0:T(8,128)(2,1)}, bf16[64,256]{1,0:T(8,128)(2,1)S(1)}, u32[]{:S(2)}, u32[]{:S(2)}) collective-permute-start(bf16[64,256]{1,0:T(8,128)(2,1)} %param.16), channel_id=1, source_target_pairs={{0,6},{2,8},{4,10},{6,12},{8,14},{10,16},{12,18},{14,20},{16,22},{... | collective-permute-start | bytes 98312 | tf_op jit(solution)/shard_map/ppermute | solution.py:20
  17.3 22.5 %collective-permute-start.6 = (bf16[64,256]{1,0:T(8,128)(2,1)}, bf16[64,256]{1,0:T(8,128)(2,1)S(1)}, u32[]{:S(2)}, u32[]{:S(2)}) collective-permute-start(bf16[64,256]{1,0:T(8,128)(2,1)} %param.16), channel_id=1, source_target_pairs={{0,4},{2,6},{4,8},{6,10},{8,12},{10,14},{12,16},{14,18},{16,20},{1... | collective-permute-start | bytes 98312 | tf_op jit(solution)/shard_map/ppermute | solution.py:20
  21.4 20.3 %collective-permute-start.7 = (bf16[64,256]{1,0:T(8,128)(2,1)}, bf16[64,256]{1,0:T(8,128)(2,1)S(1)}, u32[]{:S(2)}, u32[]{:S(2)}) collective-permute-start(bf16[64,256]{1,0:T(8,128)(2,1)} %param.16), channel_id=1, source_target_pairs={{0,2},{2,4},{4,6},{6,8},{8,10},{10,12},{12,14},{14,16},{16,18},{18... | collective-permute-start | bytes 98312 | tf_op jit(solution)/shard_map/ppermute | solution.py:20
  24.2 18.3 %collective-permute-start = (bf16[64,256]{1,0:T(8,128)(2,1)}, bf16[64,256]{1,0:T(8,128)(2,1)S(1)}, u32[]{:S(2)}, u32[]{:S(2)}) collective-permute-start(bf16[64,256]{1,0:T(8,128)(2,1)} %param.17), channel_id=1, source_target_pairs={{0,8},{2,10},{4,12},{6,14},{8,16},{10,18},{12,20},{14,22},{16,24},... | collective-permute-start | bytes 98312 | tf_op jit(solution)/shard_map/ppermute | solution.py:20
  31.6 10.9 %collective-permute-start.1 = (bf16[64,256]{1,0:T(8,128)(2,1)}, bf16[64,256]{1,0:T(8,128)(2,1)S(1)}, u32[]{:S(2)}, u32[]{:S(2)}) collective-permute-start(bf16[64,256]{1,0:T(8,128)(2,1)} %param.17), channel_id=1, source_target_pairs={{0,6},{2,8},{4,10},{6,12},{8,14},{10,16},{12,18},{14,20},{16,22},{... | collective-permute-start | bytes 98312 | tf_op jit(solution)/shard_map/ppermute | solution.py:20
  36.3 8.7 %collective-permute-start.2 = (bf16[64,256]{1,0:T(8,128)(2,1)}, bf16[64,256]{1,0:T(8,128)(2,1)S(1)}, u32[]{:S(2)}, u32[]{:S(2)}) collective-permute-start(bf16[64,256]{1,0:T(8,128)(2,1)} %param.17), channel_id=1, source_target_pairs={{0,4},{2,6},{4,8},{6,10},{8,12},{10,14},{12,16},{14,18},{16,20},{1... | collective-permute-start | bytes 98312 | tf_op jit(solution)/shard_map/ppermute | solution.py:20
  39.8 8.1 %collective-permute-start.3 = (bf16[64,256]{1,0:T(8,128)(2,1)}, bf16[64,256]{1,0:T(8,128)(2,1)S(1)}, u32[]{:S(2)}, u32[]{:S(2)}) collective-permute-start(bf16[64,256]{1,0:T(8,128)(2,1)} %param.17), channel_id=1, source_target_pairs={{0,2},{2,4},{4,6},{6,8},{8,10},{10,12},{12,14},{14,16},{16,18},{18... | collective-permute-start | bytes 98312 | tf_op jit(solution)/shard_map/ppermute | solution.py:20
  133.0 2.3 copy-start.3
  133.0 2.9 copy-start.4
  133.0 141.6 %copy-start.1 = (bf16[32,1536]{1,0:T(8,128)(2,1)S(1)}, bf16[32,1536]{1,0:T(8,128)(2,1)}, u32[]{:S(2)}) copy-start(bf16[32,1536]{1,0:T(8,128)(2,1)} %param.20) | copy-start | bytes 294916
  133.0 142.7 %copy-start.5 = (f32[1536]{0:T(1024)S(1)}, f32[1536]{0:T(1024)}, u32[]{:S(2)}) copy-start(f32[1536]{0:T(1024)} %param.21) | copy-start | bytes 18436
  134.6 278.4 %all-gather.10.cloned.1.call-start = ((), (), s32[]{:S(2)}) async-start(), calls=%async_computation.7 | async-start | bytes 3158016 | tf_op jit(solution)/shard_map/all_gather | solution.py:104
  135.2 283.7 %all-gather.6.cloned.1.call-start = ((), (), s32[]{:S(2)}) async-start(), calls=%async_computation.5 | async-start | bytes 6316032 | tf_op jit(solution)/shard_map/all_gather | solution.py:103
  285.0 101.7 %copy-start.6 = (bf16[1,1536,2,256]{3,2,1,0:T(2,128)(2,1)S(1)}, bf16[1,1536,2,256]{3,2,1,0:T(2,128)(2,1)}, u32[]{:S(2)}) copy-start(bf16[1,1536,2,256]{3,2,1,0:T(2,128)(2,1)} %param.26) | copy-start | bytes 4718596
  285.0 94.4 %all-to-all-start = ((bf16[128,1,6,1536]{3,2,1,0:T(8,128)(2,1)}), bf16[128,1,6,1536]{3,2,1,0:T(8,128)(2,1)}, u32[]{:S(2)}, u32[]{:S(2)}) async-start(bf16[128,1,6,1536]{3,2,1,0:T(8,128)(2,1)} %bitcast.347), calls=%async_computation.1 | async-start | bytes 6291456 | tf_op jit(solution)/shard_map/all_to_all | solution.py:124
  379.4 22.2 %all-to-all-start.2 = ((bf16[128,1,1,8,2,128]{5,4,3,2,1,0:T(2,128)(2,1)}), bf16[128,1,1,8,2,128]{5,4,3,2,1,0:T(2,128)(2,1)S(1)}, u32[]{:S(2)}, u32[]{:S(2)}) async-start(bf16[128,1,1,8,2,128]{5,4,3,2,1,0:T(2,128)(2,1)} %constant_dynamic-update-slice_fusion.10), calls=%async_computation.3 | async-start | bytes 1048576 | tf_op jit(solution)/shard_map/all_to_all | solution.py:55
  393.8 16.0 %copy-start.2 = (f32[32,6]{0,1:T(8,128)S(1)}, f32[32,6]{0,1:T(8,128)}, u32[]{:S(2)}) copy-start(f32[32,6]{0,1:T(8,128)} %param.23) | copy-start | bytes 2308
  393.8 16.1 %copy-start.7 = (s32[128]{0:T(128)S(1)}, s32[128]{0:T(128)}, u32[]{:S(2)}) copy-start(s32[128]{0:T(128)} %param.29) | copy-start | bytes 1540
  401.6 76.7 %all-to-all-start.1 = ((bf16[128,1,6,1536]{3,2,1,0:T(8,128)(2,1)}), bf16[128,1,6,1536]{3,2,1,0:T(8,128)(2,1)}, u32[]{:S(2)}, u32[]{:S(2)}) async-start(bf16[128,1,6,1536]{3,2,1,0:T(8,128)(2,1)} %copy.66), calls=%async_computation.2 | async-start | bytes 6291456 | tf_op jit(solution)/shard_map/all_to_all | solution.py:132
Sparse Core Ops, SparseCore 0:
  12.5 116.7 all-gather.7
  134.8 11.3 reduce-scatter.1
Sparse Core Ops, SparseCore 1:
  139.5 103.6 all-gather.9
  248.1 127.8 all-gather.5
